TPU v7x, 512 devices: a whole 4x4x16 slice. The times are simulated.
512 devices in a mesh: tiles: 128 (over z, y, core), rep: 4 (over x).
Axes of the slice: x: 4, y: 4, z: 16, core: 2. Of those that a mesh axis runs over, the one named last changes fastest.
Arguments:
- tiles: bfloat16 [1024, 64, 4096], P(('tiles', 'rep')), may hold values from -6 to 6
- block_one: int32 [1024], P(('tiles', 'rep')), may hold values from 0 to 127
- block_two: int32 [1024], P(('tiles', 'rep')), may hold values from 0 to 255
- block_three: int32 [1024], P(('tiles', 'rep')), may hold values from 0 to 15
- owner_map: int32 [128], replicated, may hold values from 0 to 127, each once
- u_one: float32 [32, 8192], P(None, 'tiles'), may hold values from -6 to 6
- u_two: bfloat16 [32, 16384], P(None, 'tiles'), may hold values from -6 to 6
- u_three: bfloat16 [32, 1024], replicated, may hold values from -6 to 6
Outputs:
- factor: float32 [32, 8192], P(None, 'tiles')
- tile_factor: bfloat16 [1024, 2048], P(('tiles', 'rep'))
All inputs are finite; a program needn't handle non-finite values.
Results may differ from a plain program's by a relative error of at most 0.0081.
Values may be sent and summed in bfloat16 or wider, within the bound.
A program may use at most 64 MiB of HBM per device.

v0:
```python
import jax
import jax.numpy as jnp
from jax import lax
from jax.sharding import PartitionSpec as P

NS_STEPS = 2


def pick(table, index, width):
    grid = table.reshape(table.shape[0], -1, width)
    return jnp.transpose(jnp.take(grid, index, axis=1), (1, 0, 2))


def gram_total(local):
    return lax.psum(local, "tiles")


def orthonormal(rows, rows_total):
    hi = lax.Precision.HIGHEST
    rank = rows.shape[0]
    g0 = gram_total(jnp.dot(rows, rows.T, precision=hi, preferred_element_type=jnp.float32))
    msq = jnp.trace(g0) / rows_total
    inv = 1.0 / jnp.sqrt(msq + 1e-06)
    x = rows * inv
    g = g0 * (inv * inv) / rows_total
    eye = jnp.eye(rank, dtype=jnp.float32)
    for step in range(NS_STEPS):
        if step > 0:
            g = (
                gram_total(jnp.dot(x, x.T, precision=hi, preferred_element_type=jnp.float32))
                / rows_total
            )
        x = jnp.dot(1.5 * eye - 0.5 * g, x, precision=hi, preferred_element_type=jnp.float32)
    return x


def spread(current):
    cast = current.astype(jnp.bfloat16)
    return lax.all_gather(cast, "tiles", axis=1, tiled=True)


def per_device(tiles, block_one, block_two, block_three, owner_map, u_one, u_two, u_three):
    hi = lax.Precision.HIGHEST
    count = tiles.shape[0]
    width = tiles.shape[1]
    rank = u_three.shape[0]
    blocks_total = owner_map.shape[0]
    rows_total = blocks_total * width
    two_full = lax.all_gather(u_two, "tiles", axis=1, tiled=True)
    two_pick = pick(two_full, block_two, width)
    three_pick = pick(u_three, block_three, width)
    cube = tiles.reshape(count, width, width, width)
    first = jnp.einsum(
        "tijk,tsk->tijs", cube, three_pick, preferred_element_type=jnp.float32
    ).astype(jnp.bfloat16)
    second = jnp.einsum("tijs,trj->tirs", first, two_pick, preferred_element_type=jnp.float32)
    products = second.reshape(count, width, rank * rank).astype(jnp.bfloat16)
    positions = jnp.take(owner_map, block_one)
    onehot = (positions[:, None] == jnp.arange(blocks_total, dtype=jnp.int32)[None, :]).astype(
        jnp.float32
    )
    current = u_one
    readers = pick(spread(current), positions, width)
    partial_value = jnp.einsum("tic,tri->rc", products, readers, preferred_element_type=jnp.float32)
    project = lax.psum(partial_value, ("tiles", "rep")).astype(jnp.bfloat16)
    z_tile = jnp.einsum("rc,tic->tri", project, products, preferred_element_type=jnp.float32)
    term = jnp.einsum("tri,tn->rni", z_tile, onehot, precision=hi).reshape(rank, rows_total)
    rows = lax.psum_scatter(term, "tiles", scatter_dimension=1, tiled=True)
    rows = lax.psum(rows, "rep")
    current = orthonormal(rows, rows_total)
    tile_factor = pick(spread(current), positions, width).reshape(count, rank * width)
    return (current, tile_factor)


def solution(mesh):
    in_specs = (
        P(("tiles", "rep"), None, None),
        P(("tiles", "rep")),
        P(("tiles", "rep")),
        P(("tiles", "rep")),
        P(),
        P(None, "tiles"),
        P(None, "tiles"),
        P(),
    )
    out_specs = (P(None, "tiles"), P(("tiles", "rep"), None))
    return jax.shard_map(
        per_device, mesh=mesh, in_specs=in_specs, out_specs=out_specs, check_vma=False
    )
```

profile of v0, /device:TPU:1, one launch (start us, length us, event | category | flops | bytes accessed | tf_op | source)
XLA Modules:
  0.0 1633.5 jit_solution(5011610970250502089)
XLA Ops:
  7.2 0.7 all-gather.4.cloned.1.call-update
  8.0 0.7 compare_select_fusion.3
  8.6 0.7 convert_bitcast_fusion.1
  9.3 1.0 reshape.51
  10.4 109.1 %all-gather = bf16[128,64,32]{1,2,0:T(8,128)(2,1)S(1)} all-gather(bf16[1,64,32]{1,2,0:T(8,128)(2,1)S(1)} %convert_bitcast_fusion.1), channel_id=1, replica_groups=mesh['tiles'=128,'rep'=4] {'tiles'}, dimensions={0}, use_global_device_ids=true | all-gather | bytes 528384 | tf_op jit(solution)/shard_map/all_gather | solution.py:39
  119.9 0.8 reshape.103
  120.7 1.1 reshape.53
  121.9 0.7 copy.32
  122.6 3.4 reshape.52
  126.1 0.6 gather_fusion
  126.7 0.6 gather_fusion.2
  128.0 2.0 fusion
  130.0 17.5 %all-gather.4.cloned.1.call-done = bf16[32,16384]{1,0:T(8,128)(2,1)} async-done(((bf16[32,128]{1,0:T(8,128)(2,1)}), bf16[32,16384]{1,0:T(8,128)(2,1)}) %all-gather.4.cloned.1.call-update) | async-done | bytes 1048592 | tf_op jit(solution)/shard_map/all_gather | solution.py:49
  147.5 3.0 reshape.50
  150.6 2.7 copy.27
  153.3 2.1 gather_fusion.1
  155.4 1.1 fusion.1
  157.0 102.8 %all-reduce.1 = bf16[32,1024]{1,0:T(8,128)(2,1)S(1)} all-reduce(f32[32,1024]{1,0:T(8,128)S(1)} %convolution_bitcast_fusion.1), channel_id=1, replica_groups=mesh['tiles'=128,'rep'=4] {'tiles','rep'}, use_global_device_ids=true, to_apply=%region_0.0 | all-reduce | flops 32768 | bytes 196608 | tf_op jit(solution)/shard_map/psum | solution.py:65
  259.9 1.0 convolution_bitcast_fusion
  261.0 4.4 copy.45
  265.5 245.9 %reduce-scatter.4.cloned.1.call-done = f32[64,32]{1,0:T(8,128)} async-done(((f32[8192,32]{1,0:T(8,128)}), f32[64,32]{1,0:T(8,128)}) %reduce-scatter.4.cloned.1.call-update) | async-done | bytes 8208
  511.3 0.8 copy.44
  512.2 13.3 psum.29
  525.6 500.6 %psum.30 = f32[32,32]{1,0:T(8,128)S(1)} all-reduce(f32[32,32]{1,0:T(8,128)S(1)} %fusion.44), channel_id=1, replica_groups=mesh['tiles'=128,'rep'=4] {'tiles'}, use_global_device_ids=true, to_apply=%region_3.5 | all-reduce | flops 1024 | bytes 8192 | tf_op jit(solution)/shard_map/psum | solution.py:15
  1026.3 0.6 select_reduce_fusion
  1027.9 490.9 %psum.31 = f32[32,32]{1,0:T(8,128)S(1)} all-reduce(f32[32,32]{1,0:T(8,128)S(1)} %fusion.45), channel_id=1, replica_groups=mesh['tiles'=128,'rep'=4] {'tiles'}, use_global_device_ids=true, to_apply=%region_5.7 | all-reduce | flops 1024 | bytes 8192 | tf_op jit(solution)/shard_map/psum | solution.py:15
  1518.9 103.3 %all-gather.1 = bf16[128,64,32]{1,2,0:T(8,128)(2,1)S(1)} all-gather(bf16[1,64,32]{1,2,0:T(8,128)(2,1)S(1)} %convert_bitcast_fusion), channel_id=1, replica_groups=mesh['tiles'=128,'rep'=4] {'tiles'}, dimensions={0}, use_global_device_ids=true | all-gather | bytes 528384 | tf_op jit(solution)/shard_map/all_gather | solution.py:39
  1622.6 0.8 reshape.105
  1623.5 1.1 reshape.55
  1624.6 0.7 copy.38
  1625.3 0.6 gather_fusion.4
  1625.9 0.7 reshape.56
  (36 shorter events, 2.9 us)
Async XLA Ops:
  7.2 118.9 %copy-start = (s32[128]{0:T(128)S(1)}, s32[128]{0:T(128)}, u32[]{:S(2)}) copy-start(s32[128]{0:T(128)} %param.14) | copy-start | bytes 1540
  7.2 140.3 %all-gather.4.cloned.1.call-start = ((), (), s32[]{:S(2)}) async-start(), calls=%async_computation.1 | async-start | bytes 1056768 | tf_op jit(solution)/shard_map/all_gather | solution.py:49
  7.9 503.4 %reduce-scatter.4.cloned.1.call-start = ((), (), s32[]{:S(2)}) async-start(), calls=%async_computation.2 | async-start | bytes 4227072
  122.6 4.2 copy-start.4
  122.6 4.7 copy-start.2
  122.6 5.3 copy-start.3
  1518.9 104.6 %copy-start.1 = (f32[32,64]{1,0:T(8,128)}, f32[32,64]{1,0:T(8,128)S(1)}, u32[]{:S(2)}) copy-start(f32[32,64]{1,0:T(8,128)S(1)} %fusion.7) | copy-start | bytes 24580
Sparse Core Ops, SparseCore 0:
  11.0 136.4 all-gather.3
  265.6 245.7 reduce-scatter.3
where the time goes:
time: 1630 us
  blocking collectives  1320 us (81%)
  waiting for transfers between devices  264 us (16%)
  local copies, waits for them, and re-layouts  27 us (2%)
    psum x2, blocking collectives, gram_total(): return lax.psum(local, 'tiles')  992 us
    unnamed x3, waiting for transfers between devices  247 us
    all_gather x2, blocking collectives, spread(): return lax.all_gather(cast, 'tiles', axis=1, tiled=True)  212 us
    psum x1, blocking collectives, per_device(): project = lax.psum(partial_value, ('tiles', 'rep')).astype(jnp.bfloat16)  103 us
  transfers between devices with their start and end apart: 2, of which 2 were waited for; matrix products, arithmetic and copies ran while one was open for 1% of the time, Pallas kernels for 0%

commit v1 on v0

--- a/solution.py
+++ b/solution.py
@@ -62,7 +62,8 @@
     current = u_one
     readers = pick(spread(current), positions, width)
     partial_value = jnp.einsum("tic,tri->rc", products, readers, preferred_element_type=jnp.float32)
-    project = lax.psum(partial_value, ("tiles", "rep")).astype(jnp.bfloat16)
+    _close_clusters = lambda x_part: jax.lax.psum(jax.lax.psum(x_part, "rep"), "tiles")
+    project = _close_clusters(partial_value).astype(jnp.bfloat16)
     z_tile = jnp.einsum("rc,tic->tri", project, products, preferred_element_type=jnp.float32)
     term = jnp.einsum("tri,tn->rni", z_tile, onehot, precision=hi).reshape(rank, rows_total)
     rows = lax.psum_scatter(term, "tiles", scatter_dimension=1, tiled=True)

time: 1630 us -> 2080 us (1.28)
  blocking collectives: 1320 us -> 1710 us
  waiting for transfers between devices: 264 us -> 322 us
    psum x1, blocking collectives: 103 us -> 491 us  [per_device(): jax.lax.psum(jax.lax.psum(x_part, 'rep'), 'tiles')]
    psum x0 -> x1, waiting for transfers between devices: none -> 49.8 us  [per_device(): jax.lax.psum(x_part, 'rep')]
    unnamed x3 -> x4, waiting for transfers between devices: 247 us -> 255 us
  transfers between devices with their start and end apart: 2 -> 3, of which waited for: 2 -> 3; matrix products, arithmetic and copies ran while one was open for 1% -> 1% of each run, Pallas kernels for 0% -> 0%
where the time goes in v1:
time: 2080 us
  blocking collectives  1710 us (82%)
  waiting for transfers between devices  322 us (15%)
  local copies, waits for them, and re-layouts  27 us (1%)
    psum x2, blocking collectives, gram_total(): return lax.psum(local, 'tiles')  991 us
    psum x1, blocking collectives, per_device(): jax.lax.psum(jax.lax.psum(x_part, 'rep'), 'tiles')  491 us
    unnamed x4, waiting for transfers between devices  255 us
    all_gather x2, blocking collectives, spread(): return lax.all_gather(cast, 'tiles', axis=1, tiled=True)  212 us
    psum x1, waiting for transfers between devices, per_device(): jax.lax.psum(x_part, 'rep')  49.8 us
  transfers between devices with their start and end apart: 3, of which 3 were waited for; matrix products, arithmetic and copies ran while one was open for 1% of the time, Pallas kernels for 0%

profile of v1, /device:TPU:1, one launch (start us, length us, event | category | flops | bytes accessed | tf_op | source)
XLA Modules:
  0.0 2080.5 jit_solution(5322688300808266680)
XLA Ops:
  7.2 0.7 all-gather.4.cloned.1.call-update
  8.0 0.7 compare_select_fusion.3
  8.6 0.7 convert_bitcast_fusion.1
  9.3 1.0 reshape.51
  10.4 109.1 %all-gather = bf16[128,64,32]{1,2,0:T(8,128)(2,1)S(1)} all-gather(bf16[1,64,32]{1,2,0:T(8,128)(2,1)S(1)} %convert_bitcast_fusion.1), channel_id=1, replica_groups=mesh['tiles'=128,'rep'=4] {'tiles'}, dimensions={0}, use_global_device_ids=true | all-gather | bytes 528384 | tf_op jit(solution)/shard_map/all_gather | solution.py:39
  119.9 0.8 reshape.103
  120.7 1.1 reshape.53
  121.9 0.7 copy.32
  122.6 3.4 reshape.52
  126.1 0.6 gather_fusion
  128.0 2.0 fusion
  130.0 17.5 all-gather.4.cloned.1.call-done
  147.5 3.0 reshape.50
  150.6 2.7 copy.27
  153.3 2.1 gather_fusion.1
  155.4 1.1 fusion.1
  156.7 0.9 convolution_bitcast_fusion.1
  157.7 49.8 %all-reduce.3.cloned.1.call-done = f32[32,1024]{1,0:T(8,128)} async-done(((f32[32,1024]{1,0:T(8,128)}), f32[32,1024]{1,0:T(8,128)}) %all-reduce.3.cloned.1.call-update) | async-done | bytes 131088 | tf_op jit(solution)/shard_map/psum | solution.py:65
  207.5 491.5 %all-reduce.4 = bf16[32,1024]{1,0:T(8,128)(2,1)S(1)} all-reduce(f32[32,1024]{1,0:T(8,128)} %all-reduce.3.cloned.1.call-done), channel_id=1, replica_groups=mesh['tiles'=128,'rep'=4] {'tiles'}, use_global_device_ids=true, to_apply=%region_1.3 | all-reduce | flops 32768 | bytes 196608 | tf_op jit(solution)/shard_map/psum | solution.py:65
  699.2 1.0 convolution_bitcast_fusion
  700.3 4.4 copy.45
  704.7 253.9 %reduce-scatter.4.cloned.1.call-done = f32[64,32]{1,0:T(8,128)} async-done(((f32[8192,32]{1,0:T(8,128)}), f32[64,32]{1,0:T(8,128)}) %reduce-scatter.4.cloned.1.call-update) | async-done | bytes 8208
  958.7 0.8 copy.44
  959.5 13.4 psum.37
  973.0 500.6 %psum.38 = f32[32,32]{1,0:T(8,128)S(1)} all-reduce(f32[32,32]{1,0:T(8,128)S(1)} %fusion.44), channel_id=1, replica_groups=mesh['tiles'=128,'rep'=4] {'tiles'}, use_global_device_ids=true, to_apply=%region_4.6 | all-reduce | flops 1024 | bytes 8192 | tf_op jit(solution)/shard_map/psum | solution.py:15
  1473.6 0.6 select_reduce_fusion
  1475.2 490.9 %psum.39 = f32[32,32]{1,0:T(8,128)S(1)} all-reduce(f32[32,32]{1,0:T(8,128)S(1)} %fusion.45), channel_id=1, replica_groups=mesh['tiles'=128,'rep'=4] {'tiles'}, use_global_device_ids=true, to_apply=%region_6.8 | all-reduce | flops 1024 | bytes 8192 | tf_op jit(solution)/shard_map/psum | solution.py:15
  1966.3 103.3 %all-gather.1 = bf16[128,64,32]{1,2,0:T(8,128)(2,1)S(1)} all-gather(bf16[1,64,32]{1,2,0:T(8,128)(2,1)S(1)} %convert_bitcast_fusion), channel_id=1, replica_groups=mesh['tiles'=128,'rep'=4] {'tiles'}, dimensions={0}, use_global_device_ids=true | all-gather | bytes 528384 | tf_op jit(solution)/shard_map/all_gather | solution.py:39
  2070.0 0.8 reshape.105
  2070.8 1.1 reshape.55
  2072.0 0.7 copy.38
  2073.3 0.7 reshape.56
  (39 shorter events, 3.8 us)
Async XLA Ops:
  7.2 118.9 %copy-start = (s32[128]{0:T(128)S(1)}, s32[128]{0:T(128)}, u32[]{:S(2)}) copy-start(s32[128]{0:T(128)} %param.14) | copy-start | bytes 1540
  7.2 140.3 %all-gather.4.cloned.1.call-start = ((), (), s32[]{:S(2)}) async-start(), calls=%async_computation.1 | async-start | bytes 1056768 | tf_op jit(solution)/shard_map/all_gather | solution.py:49
  7.9 199.6 %all-reduce.3.cloned.1.call-start = ((), (), s32[]{:S(2)}) async-start(), calls=%async_computation.2 | async-start | bytes 262144 | tf_op jit(solution)/shard_map/psum | solution.py:65
  122.6 4.2 copy-start.4
  122.6 4.7 copy-start.2
  122.6 5.3 copy-start.3
  157.7 801.0 %reduce-scatter.4.cloned.1.call-start = ((), (), s32[]{:S(2)}) async-start(), calls=%async_computation.3 | async-start | bytes 4227072
  1966.2 104.6 %copy-start.1 = (f32[32,64]{1,0:T(8,128)}, f32[32,64]{1,0:T(8,128)S(1)}, u32[]{:S(2)}) copy-start(f32[32,64]{1,0:T(8,128)S(1)} %fusion.7) | copy-start | bytes 24580
Sparse Core Ops, SparseCore 0:
  11.0 136.4 all-gather.3
  157.8 49.6 all-reduce.2
  704.9 253.7 reduce-scatter.3
